TPU v7x, 32 devices: a whole 2x2x4 slice. The times are simulated.
32 devices in a mesh: seq: 8 (over z, x), head: 4 (over y, core).
Axes of the slice: x: 2, y: 2, z: 4, core: 2. Of those that a mesh axis runs over, the one named last changes fastest.
Arguments:
- inputs: bfloat16 [3, 4096, 4096], P(None, 'seq', 'head'), may hold values from -11 to 11
- conv_weight: float32 [3, 3, 4096], P(None, None, 'head'), may hold values from -9 to 9
- gain: float32 [4096], P('head'), may hold values from 0.5 to 1.5
- cotangent: bfloat16 [4096, 4096], P('seq', 'head'), may hold values from -11 to 11
Outputs:
- output: bfloat16 [4096, 4096], P('seq', 'head')
- grad_inputs: bfloat16 [3, 4096, 4096], P(None, 'seq', 'head')
All inputs are finite; a program needn't handle non-finite values.
Results may differ from a plain program's by a relative error of at most 0.0078.
Values may be sent and summed in bfloat16 or wider, within the bound.
A program may use at most 128 MiB of HBM per device.

v0:
```python
import jax
import jax.numpy as jnp
from jax import lax
from jax.sharding import PartitionSpec as P

WIDTH = 4096
HEAD_DIM = 128
BLOCK = 512


def from_behind(x, axis, by):
    devices = lax.axis_size(axis)
    pairs = [(i, i + by) for i in range(devices) if 0 <= i + by < devices]
    return lax.ppermute(x, axis, pairs)


def entering(part, axis, combine, identity, reverse):
    count = lax.axis_size(axis)
    place = lax.axis_index(axis)
    ahead = count - 1 - place if reverse else place
    gathered = lax.all_gather(part, axis)
    state = jnp.zeros_like(part) + jnp.asarray(identity, part.dtype)

    def one(step, state):
        source = count - 1 - step if reverse else step
        return combine(state, lax.dynamic_index_in_dim(gathered, source, 0, False))

    return lax.fori_loop(0, ahead, one, state)


def add_states(earlier, later):
    return earlier + later


def body(inputs, conv_weight, gain, cotangent):
    row_count = inputs.shape[1]
    col_count = inputs.shape[2]
    tap_count = conv_weight.shape[1]
    local_heads = col_count // HEAD_DIM
    block_count = row_count // BLOCK
    left_rim = from_behind(inputs[:, row_count - (tap_count - 1) :, :], "seq", 1)
    extended = jnp.concatenate([left_rim, inputs], axis=1).astype(jnp.float32)
    conv_total = jnp.zeros((3, row_count, col_count), jnp.float32)
    for offset in range(tap_count):
        start_row = tap_count - 1 - offset
        conv_total = (
            conv_total
            + conv_weight[:, offset, None, :] * extended[:, start_row : start_row + row_count, :]
        )
    convolved = conv_total.astype(jnp.bfloat16)

    def by_blocks(array):
        return array.reshape(block_count, BLOCK, local_heads, HEAD_DIM)

    queries = by_blocks(convolved[0])
    key_rows = by_blocks(convolved[1])
    values = by_blocks(convolved[2])
    causal = lax.broadcasted_iota(jnp.int32, (BLOCK, BLOCK), 0) >= lax.broadcasted_iota(
        jnp.int32, (BLOCK, BLOCK), 1
    )
    block_states = jnp.einsum(
        "nshd,nshe->nhde", key_rows, values, preferred_element_type=jnp.float32
    )
    device_state = jnp.sum(block_states, axis=0)
    zero_state = jnp.zeros_like(device_state)
    incoming = entering(device_state, "seq", add_states, zero_state, False)
    state = incoming[None] + jnp.cumsum(block_states, axis=0) - block_states
    state_bf = state.astype(jnp.bfloat16)
    scores = jnp.einsum("nthd,nshd->nhts", queries, key_rows, preferred_element_type=jnp.float32)
    scores = jnp.where(causal[None, None], scores, 0.0).astype(jnp.bfloat16)
    attended = jnp.einsum("nthd,nhde->nthe", queries, state_bf, preferred_element_type=jnp.float32)
    attended = attended + jnp.einsum(
        "nhts,nshe->nthe", scores, values, preferred_element_type=jnp.float32
    )
    attended = attended.reshape(row_count, col_count)
    weighted = gain[None, :] * cotangent.astype(jnp.float32)
    squares = jnp.sum(attended * attended, axis=-1)
    total_sq = lax.psum(squares, "head")
    rms = jnp.sqrt(total_sq / WIDTH + 1e-05)
    output = (gain[None, :] * attended / rms[:, None]).astype(jnp.bfloat16)
    inner = lax.psum(jnp.sum(weighted * attended, axis=-1), "head")
    grad_attended = (
        weighted / rms[:, None] - attended * (inner / (WIDTH * rms * rms * rms))[:, None]
    ).astype(jnp.bfloat16)
    grad_blocks = by_blocks(grad_attended)
    block_grads = jnp.einsum(
        "nthd,nthe->nhde", queries, grad_blocks, preferred_element_type=jnp.float32
    )
    device_grad = jnp.sum(block_grads, axis=0)
    later_grad = entering(device_grad, "seq", add_states, zero_state, True)
    after = later_grad[None] + device_grad[None] - jnp.cumsum(block_grads, axis=0)
    after_bf = after.astype(jnp.bfloat16)
    mixed = jnp.einsum("nthe,nshe->nhts", grad_blocks, values, preferred_element_type=jnp.float32)
    mixed = jnp.where(causal[None, None], mixed, 0.0).astype(jnp.bfloat16)
    grad_q = jnp.einsum(
        "nthe,nhde->nthd", grad_blocks, state_bf, preferred_element_type=jnp.float32
    )
    grad_q = grad_q + jnp.einsum(
        "nhts,nshd->nthd", mixed, key_rows, preferred_element_type=jnp.float32
    )
    grad_k = jnp.einsum("nshe,nhde->nshd", values, after_bf, preferred_element_type=jnp.float32)
    grad_k = grad_k + jnp.einsum(
        "nhts,nthd->nshd", mixed, queries, preferred_element_type=jnp.float32
    )
    grad_v = jnp.einsum("nshd,nhde->nshe", key_rows, after_bf, preferred_element_type=jnp.float32)
    grad_v = grad_v + jnp.einsum(
        "nhts,nthe->nshe", scores, grad_blocks, preferred_element_type=jnp.float32
    )
    grad_u = (
        jnp.stack([grad_q, grad_k, grad_v]).reshape(3, row_count, col_count).astype(jnp.bfloat16)
    )
    right_rim = from_behind(grad_u[:, : tap_count - 1, :], "seq", -1)
    extended_grad = jnp.concatenate([grad_u, right_rim], axis=1).astype(jnp.float32)
    grad_total_in = jnp.zeros((3, row_count, col_count), jnp.float32)
    for offset in range(tap_count):
        grad_total_in = (
            grad_total_in
            + conv_weight[:, offset, None, :] * extended_grad[:, offset : offset + row_count, :]
        )
    return (output, grad_total_in.astype(jnp.bfloat16))


def solution(mesh):
    placed = (P(None, "seq", "head"), P(None, None, "head"), P("head"), P("seq", "head"))
    return jax.shard_map(
        body,
        mesh=mesh,
        in_specs=placed,
        out_specs=(P("seq", "head"), P(None, "seq", "head")),
        check_vma=False,
    )
```

profile of v0, /device:TPU:0, one launch (start us, length us, event | category | flops | bytes accessed | tf_op | source)
XLA Modules:
  0.0 241.4 jit_solution(3161101124645385469)
XLA Ops:
  7.2 0.8 slice.46
  8.0 4.9 %collective-permute-start = (bf16[3,2,1024]{2,1,0:T(2,128)(2,1)S(1)}, bf16[3,2,1024]{2,1,0:T(2,128)(2,1)S(1)}, u32[]{:S(2)}, u32[]{:S(2)}) collective-permute-start(bf16[3,2,1024]{2,1,0:T(2,128)(2,1)S(1)} %slice.46), channel_id=1, source_target_pairs={{0,4},{4,8},{8,12},{12,16},{16,20},{20,24},{24,28},{1,5},{5,9},{9,... | collective-permute-start | bytes 36872 | tf_op jit(solution)/shard_map/ppermute | solution.py:14
  12.9 0.9 fusion.11
  13.9 4.6 %copy.44 = bf16[3,512,1024]{1,2,0:T(8,128)(2,1)} copy(bf16[3,512,1024]{2,1,0:T(8,128)(2,1)} %param.8) | data formatting | bytes 6291456 | tf_op args[0]
  18.5 0.4 copy.43
  18.9 3.6 %maximum_convert_fusion = f32[3,514,1024]{1,2,0:T(8,128)S(1)} fusion(bf16[3,512,1024]{1,2,0:T(8,128)(2,1)} %copy.44, bf16[3,2,1024]{1,2,0:T(8,128)(2,1)S(1)} %copy.43), kind=kLoop, calls=%fused_computation.16 | loop fusion | flops 6316032 | bytes 9474048 | tf_op jit(solution)/shard_map/convert_element_type | solution.py:42
  22.5 5.7 %fusion.4 = bf16[3,512,1024]{1,2,0:T(8,128)(2,1)S(1)} fusion(f32[3,514,1024]{1,2,0:T(8,128)S(1)} %maximum_convert_fusion, f32[3,1024]{1,0:T(4,128)S(1)} %get-tuple-element.117, f32[3,1024]{1,0:T(4,128)S(1)} %get-tuple-element.118, f32[3,1024]{1,0:T(4,128)S(1)} %bitcast.93), kind=kLoop, calls=%fused_computation.12 | loop fusion | flops 9437184 | bytes 22056960 | tf_op jit(solution)/shard_map/convert_element_type | solution.py:50
  28.3 0.2 fusion.10
  28.5 1.5 fusion.12
  30.1 0.1 iota_compare_fusion
  30.2 0.7 copy-done.11
  30.8 1.4 select_convert_fusion.1
  32.2 1.9 copy-done
  34.2 2.8 %fusion.13 = f32[8,128,512]{2,1,0:T(8,128)} fusion(bf16[512,8,128]{0,2,1:T(8,128)(2,1)S(1)} %bitcast.73, bf16[8,512,512]{2,1,0:T(8,128)(2,1)S(1)} %select_convert_fusion.1), kind=kOutput, calls=%fused_computation.44 | convolution fusion | flops 536870912 | bytes 7340032 | tf_op jit(solution)/shard_map/nhts,nshe->nthe/dot_general | solution.py:72
  37.0 66.3 %all-gather.5.cloned.1.call-done = f32[64,128,128]{2,1,0:T(8,128)} async-done(((f32[8,128,128]{2,1,0:T(8,128)}), f32[64,128,128]{2,1,0:T(8,128)}) %all-gather.5.cloned.1.call-update) | async-done | bytes 4194320 | tf_op jit(solution)/shard_map/all_gather | solution.py:21
  103.3 1.0 copy-done.10
  104.4 3.4 %fusion.6 = (f32[512]{0:T(512)S(1)}, f32[8,128,512]{2,1,0:T(8,128)}) fusion(f32[8,128,512]{2,1,0:T(8,128)} %fusion.13, bf16[8,128,128]{2,1,0:T(8,128)(2,1)S(1)} %fusion.7, bf16[512,8,128]{0,2,1:T(8,128)(2,1)S(1)} %bitcast.81), kind=kOutput, calls=%fused_computation.19 | convolution fusion | flops 135790080 | bytes 5507072 | tf_op jit(solution)/shard_map/nthd,nhde->nthe/dot_general | solution.py:71
  107.8 1.9 copy.50
  109.7 1.6 multiply_reduce_fusion
  111.3 5.8 %all-reduce = (f32[512]{0:T(512)S(1)}, f32[512]{0:T(512)S(1)}) all-reduce(f32[512]{0:T(512)S(1)} %get-tuple-element.115, f32[512]{0:T(512)S(1)} %multiply_reduce_fusion), channel_id=1, replica_groups=mesh['seq'=8,'head'=4] {'head'}, use_global_device_ids=true, to_apply=%region_3.4 | all-reduce | flops 1024 | bytes 8192 | tf_op jit(solution)/shard_map/psum | solution.py:78
  117.2 3.2 %subtract_convert_fusion = (bf16[512,1024]{1,0:T(8,128)(2,1)}, bf16[512,1024]{1,0:T(8,128)(2,1)}) fusion(f32[512,1024]{1,0:T(8,128)S(1)} %copy.50, bf16[512,1024]{1,0:T(8,128)(2,1)} %param.11, f32[512]{0:T(512)S(1)} %get-tuple-element.113, f32[512]{0:T(512)S(1)} %get-tuple-element.114, f32[1024]{0:T(1024)S(1)} %copy-done.12), kind=kLoop, calls=%fused_computation.23 | loop fusion | flops 4718592 | bytes 5251072 | tf_op jit(solution)/shard_map/convert_element_type | solution.py:84
  120.3 1.5 copy.76
  121.8 2.5 %fusion.15 = f32[8,128,128]{2,1,0:T(8,128)} fusion(bf16[512,8,128]{0,2,1:T(8,128)(2,1)} %bitcast.82, bf16[512,8,128]{0,2,1:T(8,128)(2,1)S(1)} %bitcast.68), kind=kOutput, calls=%fused_computation.46 | convolution fusion | flops 134217728 | bytes 2621440 | tf_op jit(solution)/shard_map/nthd,nthe->nhde/dot_general | solution.py:86
  124.3 2.4 select_convert_fusion
  126.7 1.5 fusion.14
  128.2 1.4 add_convert_fusion.2
  129.6 2.0 fusion.17
  131.7 2.1 fusion.16
  133.8 69.7 %all-gather.7.cloned.1.call-done = f32[64,128,128]{2,1,0:T(8,128)} async-done(((f32[8,128,128]{2,1,0:T(8,128)}), f32[64,128,128]{2,1,0:T(8,128)}) %all-gather.7.cloned.1.call-update) | async-done | bytes 4194320 | tf_op jit(solution)/shard_map/all_gather | solution.py:21
  203.5 8.4 %while.23 = (s32[]{:T(128)}, f32[8,128,128]{2,1,0:T(8,128)S(1)}, s32[]{:T(128)}, f32[8,8,128,128]{3,2,1,0:T(8,128)}, s32[]{:T(128)}, /*index=5*/s32[]{:T(128)}, s32[]{:T(128)}, s32[]{:T(128)}) while((s32[]{:T(128)}, f32[8,128,128]{2,1,0:T(8,128)S(1)}, s32[]{:T(128)}, f32[8,8,128,128]{3,2,1,0:T(8,128)}, s32[]{:T(128)}, /*index=5*/s32[]{:T(128)}, ...), condition=%wide.region_7.8_spmd, body=%wide.region_6.7_spmd.sunk | while | flops 131078 | bytes 1573007 | solution.py:28
  203.5 1.2 bitcast_add_fusion.5
  204.8 1.2 bitcast_add_fusion.5
  206.0 1.2 bitcast_add_fusion.5
  207.1 1.2 bitcast_add_fusion.5
  208.3 1.2 bitcast_add_fusion.5
  209.5 1.2 bitcast_add_fusion.5
  210.7 1.2 bitcast_add_fusion.5
  212.0 2.2 add_convert_fusion
  214.3 0.4 add_convert_fusion.1
  214.7 0.5 copy-done.7
  215.2 0.1 pad_maximum_fusion
  215.4 0.3 copy.61
  215.7 1.3 collective-permute-start.1
  217.0 4.3 %collective-permute-done.1 = bf16[3,2,1024]{2,1,0:T(2,128)(2,1)S(1)} collective-permute-done((bf16[3,2,1024]{2,1,0:T(2,128)(2,1)S(1)}, bf16[3,2,1024]{2,1,0:T(2,128)(2,1)S(1)}, u32[]{:S(2)}, u32[]{:S(2)}) %collective-permute-start.1) | collective-permute-done | bytes 12320 | tf_op jit(solution)/shard_map/ppermute | solution.py:14
  221.2 0.4 copy.62
  221.7 1.6 maximum_convert_fusion.1
  223.3 6.7 %fusion.1 = bf16[3,512,1024]{1,2,0:T(8,128)(2,1)} fusion(f32[3,514,1024]{1,2,0:T(8,128)S(1)} %maximum_convert_fusion.1, f32[3,1024]{1,0:T(4,128)S(1)} %get-tuple-element.117, f32[3,1024]{1,0:T(4,128)S(1)} %get-tuple-element.118, f32[3,1024]{1,0:T(4,128)S(1)} %bitcast.94), kind=kLoop, calls=%fused_computation.6 | loop fusion | flops 9437184 | bytes 22056960 | tf_op jit(solution)/shard_map/convert_element_type | solution.py:120
  229.9 4.6 %copy.63 = bf16[3,512,1024]{2,1,0:T(8,128)(2,1)} copy(bf16[3,512,1024]{1,2,0:T(8,128)(2,1)} %fusion.1) | data formatting | bytes 6291456
  (35 shorter events, 0.4 us)
Async XLA Ops:
  7.2 96.1 %all-gather.5.cloned.1.call-start = ((), (), s32[]{:S(2)}) async-start(), calls=%async_computation | async-start | bytes 4718592 | tf_op jit(solution)/shard_map/all_gather | solution.py:21
  8.0 10.5 %collective-permute-start = (bf16[3,2,1024]{2,1,0:T(2,128)(2,1)S(1)}, bf16[3,2,1024]{2,1,0:T(2,128)(2,1)S(1)}, u32[]{:S(2)}, u32[]{:S(2)}) collective-permute-start(bf16[3,2,1024]{2,1,0:T(2,128)(2,1)S(1)} %slice.46), channel_id=1, source_target_pairs={{0,4},{4,8},{8,12},{12,16},{16,20},{20,24},{24,28},{1,5},{5,9},{9,... | collective-permute-start | bytes 36872 | tf_op jit(solution)/shard_map/ppermute | solution.py:14
  28.5 3.7 %copy-start.2 = (bf16[1,512,1024]{1,2,0:T(8,128)(2,1)}, bf16[1,512,1024]{1,2,0:T(8,128)(2,1)S(1)}, u32[]{:S(2)}) copy-start(bf16[1,512,1024]{1,2,0:T(8,128)(2,1)S(1)} %get-tuple-element.105) | copy-start | bytes 3145732
  28.5 75.9 %copy-start.4 = (bf16[1,512,1024]{1,2,0:T(8,128)(2,1)}, bf16[1,512,1024]{1,2,0:T(8,128)(2,1)S(1)}, u32[]{:S(2)}) copy-start(bf16[1,512,1024]{1,2,0:T(8,128)(2,1)S(1)} %get-tuple-element.106) | copy-start | bytes 3145732
  30.0 173.5 %all-gather.7.cloned.1.call-start = ((), (), s32[]{:S(2)}) async-start(), calls=%async_computation.1 | async-start | bytes 4718592 | tf_op jit(solution)/shard_map/all_gather | solution.py:21
  30.1 0.7 copy-start.11
  32.2 1.9 copy-start
  103.3 1.0 copy-start.10
  104.4 5.3 %copy-start.12 = (f32[1024]{0:T(1024)S(1)}, f32[1024]{0:T(1024)}, u32[]{:S(2)}) copy-start(f32[1024]{0:T(1024)} %param.10) | copy-start | bytes 12292
  124.3 2.4 %copy-start.3 = (bf16[1,512,1024]{1,2,0:T(8,128)(2,1)S(1)}, bf16[1,512,1024]{1,2,0:T(8,128)(2,1)}, u32[]{:S(2)}) copy-start(bf16[1,512,1024]{1,2,0:T(8,128)(2,1)} %copy-done.2) | copy-start | bytes 3145732
  126.7 2.9 %copy-start.1 = (bf16[8,512,512]{2,1,0:T(8,128)(2,1)S(1)}, bf16[8,512,512]{2,1,0:T(8,128)(2,1)}, u32[]{:S(2)}) copy-start(bf16[8,512,512]{2,1,0:T(8,128)(2,1)} %copy-done) | copy-start | bytes 12582916
  129.6 2.1 copy-start.5
  203.5 8.5 %copy-start.9 = (f32[8,128,128]{2,1,0:T(8,128)S(1)}, f32[8,128,128]{2,1,0:T(8,128)}, u32[]{:S(2)}) copy-start(f32[8,128,128]{2,1,0:T(8,128)} %fusion.15) | copy-start | bytes 1572868
  211.9 2.3 copy-start.8
  212.0 3.2 %copy-start.6 = (bf16[8,128,512]{2,1,0:T(8,128)(2,1)S(1)}, bf16[8,128,512]{2,1,0:T(8,128)(2,1)}, u32[]{:S(2)}) copy-start(bf16[8,128,512]{2,1,0:T(8,128)(2,1)} %add_convert_fusion.2) | copy-start | bytes 3145732
  214.2 1.0 copy-start.7
  215.7 5.6 %collective-permute-start.1 = (bf16[3,2,1024]{2,1,0:T(2,128)(2,1)S(1)}, bf16[3,2,1024]{2,1,0:T(2,128)(2,1)S(1)}, u32[]{:S(2)}, u32[]{:S(2)}) collective-permute-start(bf16[3,2,1024]{2,1,0:T(2,128)(2,1)S(1)} %copy.61), channel_id=1, source_target_pairs={{4,0},{8,4},{12,8},{16,12},{20,16},{24,20},{28,24},{5,1},{9,5},{13... | collective-permute-start | bytes 36872 | tf_op jit(solution)/shard_map/ppermute | solution.py:14
Sparse Core Ops, SparseCore 0:
  30.1 73.0 all-gather.4
  124.4 78.9 all-gather.6
where the time goes:
time: 242 us; the launch traced here: 241 us
  waiting for transfers between devices  140 us (58%)
  other arithmetic  30.9 us (13%)
  matrix products  23.6 us (10%)
  local copies, waits for them, and re-layouts  20 us (8%)
  between operations  14.3 us (6%)
  starting transfers between devices  6.24 us (3%)
  blocking collectives  5.85 us (2%)
    all_gather x2, waiting for transfers between devices, entering(): gathered = lax.all_gather(part, axis)  136 us
    unnamed x30, local copies, waits for them, and re-layouts  13.4 us
    add x7, other arithmetic, add_states(): return earlier + later  8.23 us
    convert_element_type x1, other arithmetic, body(): return (output, grad_total_in.astype(jnp.bfloat16))  6.65 us
    ppermute x2, starting transfers between devices, from_behind(): return lax.ppermute(x, axis, pairs)  6.16 us
    psum x1, blocking collectives, body(): total_sq = lax.psum(squares, 'head')  5.85 us
    convert_element_type x1, other arithmetic, body(): convolved = conv_total.astype(jnp.bfloat16)  5.72 us
  transfers between devices with their start and end apart: 4, of which 3 were waited for; matrix products, arithmetic and copies ran while one was open for 8% of the time, Pallas kernels for 0%

commit v1 on v0

--- a/solution.py
+++ b/solution.py
@@ -75,7 +75,7 @@
     attended = attended.reshape(row_count, col_count)
     weighted = gain[None, :] * cotangent.astype(jnp.float32)
     squares = jnp.sum(attended * attended, axis=-1)
-    total_sq = lax.psum(squares, "head")
+    total_sq = jnp.sum(lax.all_gather(squares, "head"), axis=0)
     rms = jnp.sqrt(total_sq / WIDTH + 1e-05)
     output = (gain[None, :] * attended / rms[:, None]).astype(jnp.bfloat16)
     inner = lax.psum(jnp.sum(weighted * attended, axis=-1), "head")

time: 242 us -> 248 us (1.025)
  blocking collectives: 5.85 us -> 11 us
    all_gather x0 -> x1, blocking collectives: none -> 5.36 us  [body(): total_sq = jnp.sum(lax.all_gather(squares, 'head'), axis=0)]
where the time goes in v1:
time: 248 us; the launch traced here: 247 us
  waiting for transfers between devices  140 us (56%)
  other arithmetic  30.9 us (12%)
  matrix products  23.6 us (10%)
  local copies, waits for them, and re-layouts  20 us (8%)
  between operations  14.3 us (6%)
  blocking collectives  11 us (4%)
  starting transfers between devices  6.24 us (3%)
    all_gather x2, waiting for transfers between devices, entering(): gathered = lax.all_gather(part, axis)  136 us
    unnamed x30, local copies, waits for them, and re-layouts  13.5 us
    add x7, other arithmetic, add_states(): return earlier + later  8.23 us
    convert_element_type x1, other arithmetic, body(): return (output, grad_total_in.astype(jnp.bfloat16))  6.64 us
    ppermute x2, starting transfers between devices, from_behind(): return lax.ppermute(x, axis, pairs)  6.16 us
    convert_element_type x1, other arithmetic, body(): convolved = conv_total.astype(jnp.bfloat16)  5.72 us
    psum x1, blocking collectives, body(): inner = lax.psum(jnp.sum(weighted * attended, axis=-1), 'head')  5.66 us
    all_gather x1, blocking collectives, body(): total_sq = jnp.sum(lax.all_gather(squares, 'head'), axis=0)  5.36 us
  transfers between devices with their start and end apart: 4, of which 3 were waited for; matrix products, arithmetic and copies ran while one was open for 8% of the time, Pallas kernels for 0%

profile of v1, /device:TPU:0, one launch (start us, length us, event | category | flops | bytes accessed | tf_op | source)
XLA Modules:
  0.0 246.6 jit_solution(17428833264811282642)
XLA Ops:
  7.2 0.8 slice.46
  8.0 4.9 %collective-permute-start = (bf16[3,2,1024]{2,1,0:T(2,128)(2,1)S(1)}, bf16[3,2,1024]{2,1,0:T(2,128)(2,1)S(1)}, u32[]{:S(2)}, u32[]{:S(2)}) collective-permute-start(bf16[3,2,1024]{2,1,0:T(2,128)(2,1)S(1)} %slice.46), channel_id=1, source_target_pairs={{0,4},{4,8},{8,12},{12,16},{16,20},{20,24},{24,28},{1,5},{5,9},{9,... | collective-permute-start | bytes 36872 | tf_op jit(solution)/shard_map/ppermute | solution.py:14
  12.9 0.9 fusion.11
  13.9 4.6 %copy.44 = bf16[3,512,1024]{1,2,0:T(8,128)(2,1)} copy(bf16[3,512,1024]{2,1,0:T(8,128)(2,1)} %param.8) | data formatting | bytes 6291456 | tf_op args[0]
  18.5 0.4 copy.43
  18.9 3.6 %maximum_convert_fusion = f32[3,514,1024]{1,2,0:T(8,128)S(1)} fusion(bf16[3,512,1024]{1,2,0:T(8,128)(2,1)} %copy.44, bf16[3,2,1024]{1,2,0:T(8,128)(2,1)S(1)} %copy.43), kind=kLoop, calls=%fused_computation.16 | loop fusion | flops 6316032 | bytes 9474048 | tf_op jit(solution)/shard_map/convert_element_type | solution.py:42
  22.5 5.7 %fusion.4 = bf16[3,512,1024]{1,2,0:T(8,128)(2,1)S(1)} fusion(f32[3,514,1024]{1,2,0:T(8,128)S(1)} %maximum_convert_fusion, f32[3,1024]{1,0:T(4,128)S(1)} %get-tuple-element.115, f32[3,1024]{1,0:T(4,128)S(1)} %get-tuple-element.116, f32[3,1024]{1,0:T(4,128)S(1)} %bitcast.94), kind=kLoop, calls=%fused_computation.12 | loop fusion | flops 9437184 | bytes 22056960 | tf_op jit(solution)/shard_map/convert_element_type | solution.py:50
  28.3 0.2 fusion.10
  28.5 1.5 fusion.12
  30.2 0.7 copy-done.11
  30.8 1.4 select_convert_fusion.1
  32.2 2.0 copy-done
  34.2 2.8 %fusion.13 = f32[8,128,512]{2,1,0:T(8,128)} fusion(bf16[512,8,128]{0,2,1:T(8,128)(2,1)S(1)} %bitcast.74, bf16[8,512,512]{2,1,0:T(8,128)(2,1)S(1)} %select_convert_fusion.1), kind=kOutput, calls=%fused_computation.44 | convolution fusion | flops 536870912 | bytes 7340032 | tf_op jit(solution)/shard_map/nhts,nshe->nthe/dot_general | solution.py:72
  37.0 66.3 %all-gather.7.cloned.1.call-done = f32[64,128,128]{2,1,0:T(8,128)} async-done(((f32[8,128,128]{2,1,0:T(8,128)}), f32[64,128,128]{2,1,0:T(8,128)}) %all-gather.7.cloned.1.call-update) | async-done | bytes 4194320 | tf_op jit(solution)/shard_map/all_gather | solution.py:21
  103.3 1.0 copy-done.10
  104.4 3.4 %fusion.6 = (f32[512]{0:T(512)S(1)}, f32[8,128,512]{2,1,0:T(8,128)}) fusion(f32[8,128,512]{2,1,0:T(8,128)} %fusion.13, bf16[8,128,128]{2,1,0:T(8,128)(2,1)S(1)} %fusion.7, bf16[512,8,128]{0,2,1:T(8,128)(2,1)S(1)} %bitcast.82), kind=kOutput, calls=%fused_computation.19 | convolution fusion | flops 135790080 | bytes 5507072 | tf_op jit(solution)/shard_map/nthd,nhde->nthe/dot_general | solution.py:71
  107.8 1.9 copy.50
  109.7 1.6 multiply_reduce_fusion
  111.3 5.7 %psum.7 = f32[512]{0:T(512)S(1)} all-reduce(f32[512]{0:T(512)S(1)} %multiply_reduce_fusion), channel_id=1, replica_groups=mesh['seq'=8,'head'=4] {'head'}, use_global_device_ids=true, to_apply=%region_5.6 | all-reduce | flops 512 | bytes 4096 | tf_op jit(solution)/shard_map/psum | solution.py:81
  117.0 5.4 %all-gather.3 = f32[4,1,512]{2,1,0:T(1,128)S(1)} all-gather(f32[1,1,512]{2,1,0:T(1,128)S(1)} %bitcast.96), channel_id=3, replica_groups=mesh['seq'=8,'head'=4] {'head'}, dimensions={0}, use_global_device_ids=true | all-gather | bytes 10240 | tf_op jit(solution)/shard_map/all_gather | solution.py:78
  122.4 3.2 %subtract_convert_fusion = (bf16[512,1024]{1,0:T(8,128)(2,1)}, bf16[512,1024]{1,0:T(8,128)(2,1)}) fusion(f32[512,1024]{1,0:T(8,128)S(1)} %copy.50, bf16[512,1024]{1,0:T(8,128)(2,1)} %param.11, f32[512]{0:T(512)S(1)} %get-tuple-element.111, f32[512]{0:T(512)S(1)} %get-tuple-element.112, f32[1024]{0:T(1024)S(1)} %copy-done.12), kind=kLoop, calls=%fused_computation.23 | loop fusion | flops 4718592 | bytes 5251072 | tf_op jit(solution)/shard_map/convert_element_type | solution.py:84
  125.6 1.5 copy.76
  127.1 2.5 fusion.15
  129.5 2.4 select_convert_fusion
  132.0 1.5 fusion.14
  133.5 1.4 add_convert_fusion.2
  134.9 2.0 fusion.17
  136.9 2.1 fusion.16
  139.0 69.7 %all-gather.9.cloned.1.call-done = f32[64,128,128]{2,1,0:T(8,128)} async-done(((f32[8,128,128]{2,1,0:T(8,128)}), f32[64,128,128]{2,1,0:T(8,128)}) %all-gather.9.cloned.1.call-update) | async-done | bytes 4194320 | tf_op jit(solution)/shard_map/all_gather | solution.py:21
  208.7 8.4 %while.23 = (s32[]{:T(128)}, f32[8,128,128]{2,1,0:T(8,128)S(1)}, s32[]{:T(128)}, f32[8,8,128,128]{3,2,1,0:T(8,128)}, s32[]{:T(128)}, /*index=5*/s32[]{:T(128)}, s32[]{:T(128)}, s32[]{:T(128)}) while((s32[]{:T(128)}, f32[8,128,128]{2,1,0:T(8,128)S(1)}, s32[]{:T(128)}, f32[8,8,128,128]{3,2,1,0:T(8,128)}, s32[]{:T(128)}, /*index=5*/s32[]{:T(128)}, ...), condition=%wide.region_7.8_spmd, body=%wide.region_6.7_spmd.sunk | while | flops 131078 | bytes 1573007 | solution.py:28
  208.7 1.2 bitcast_add_fusion.5
  210.0 1.2 bitcast_add_fusion.5
  211.2 1.2 bitcast_add_fusion.5
  212.4 1.2 bitcast_add_fusion.5
  213.6 1.2 bitcast_add_fusion.5
  214.7 1.2 bitcast_add_fusion.5
  215.9 1.2 bitcast_add_fusion.5
  217.2 2.2 add_convert_fusion
  219.5 0.4 add_convert_fusion.1
  219.9 0.5 copy-done.7
  220.4 0.1 pad_maximum_fusion
  220.6 0.3 copy.61
  220.9 1.3 collective-permute-start.1
  222.2 4.3 %collective-permute-done.1 = bf16[3,2,1024]{2,1,0:T(2,128)(2,1)S(1)} collective-permute-done((bf16[3,2,1024]{2,1,0:T(2,128)(2,1)S(1)}, bf16[3,2,1024]{2,1,0:T(2,128)(2,1)S(1)}, u32[]{:S(2)}, u32[]{:S(2)}) %collective-permute-start.1) | collective-permute-done | bytes 12320 | tf_op jit(solution)/shard_map/ppermute | solution.py:14
  226.5 0.4 copy.62
  226.9 1.6 maximum_convert_fusion.1
  228.5 6.6 %fusion.1 = bf16[3,512,1024]{1,2,0:T(8,128)(2,1)} fusion(f32[3,514,1024]{1,2,0:T(8,128)S(1)} %maximum_convert_fusion.1, f32[3,1024]{1,0:T(4,128)S(1)} %get-tuple-element.115, f32[3,1024]{1,0:T(4,128)S(1)} %get-tuple-element.116, f32[3,1024]{1,0:T(4,128)S(1)} %bitcast.95), kind=kLoop, calls=%fused_computation.6 | loop fusion | flops 9437184 | bytes 22056960 | tf_op jit(solution)/shard_map/convert_element_type | solution.py:120
  235.1 4.6 %copy.63 = bf16[3,512,1024]{2,1,0:T(8,128)(2,1)} copy(bf16[3,512,1024]{1,2,0:T(8,128)(2,1)} %fusion.1) | data formatting | bytes 6291456
  (37 shorter events, 0.5 us)
Async XLA Ops:
  7.2 96.1 %all-gather.7.cloned.1.call-start = ((), (), s32[]{:S(2)}) async-start(), calls=%async_computation | async-start | bytes 4718592 | tf_op jit(solution)/shard_map/all_gather | solution.py:21
  8.0 10.5 %collective-permute-start = (bf16[3,2,1024]{2,1,0:T(2,128)(2,1)S(1)}, bf16[3,2,1024]{2,1,0:T(2,128)(2,1)S(1)}, u32[]{:S(2)}, u32[]{:S(2)}) collective-permute-start(bf16[3,2,1024]{2,1,0:T(2,128)(2,1)S(1)} %slice.46), channel_id=1, source_target_pairs={{0,4},{4,8},{8,12},{12,16},{16,20},{20,24},{24,28},{1,5},{5,9},{9,... | collective-permute-start | bytes 36872 | tf_op jit(solution)/shard_map/ppermute | solution.py:14
  28.5 3.7 %copy-start.2 = (bf16[1,512,1024]{1,2,0:T(8,128)(2,1)}, bf16[1,512,1024]{1,2,0:T(8,128)(2,1)S(1)}, u32[]{:S(2)}) copy-start(bf16[1,512,1024]{1,2,0:T(8,128)(2,1)S(1)} %get-tuple-element.103) | copy-start | bytes 3145732
  28.5 75.9 %copy-start.4 = (bf16[1,512,1024]{1,2,0:T(8,128)(2,1)}, bf16[1,512,1024]{1,2,0:T(8,128)(2,1)S(1)}, u32[]{:S(2)}) copy-start(bf16[1,512,1024]{1,2,0:T(8,128)(2,1)S(1)} %get-tuple-element.104) | copy-start | bytes 3145732
  30.0 178.7 %all-gather.9.cloned.1.call-start = ((), (), s32[]{:S(2)}) async-start(), calls=%async_computation.1 | async-start | bytes 4718592 | tf_op jit(solution)/shard_map/all_gather | solution.py:21
  30.1 0.7 copy-start.11
  32.2 2.0 copy-start
  103.3 1.0 copy-start.10
  104.4 5.3 %copy-start.12 = (f32[1024]{0:T(1024)S(1)}, f32[1024]{0:T(1024)}, u32[]{:S(2)}) copy-start(f32[1024]{0:T(1024)} %param.10) | copy-start | bytes 12292
  129.5 2.4 copy-start.3
  132.0 2.9 %copy-start.1 = (bf16[8,512,512]{2,1,0:T(8,128)(2,1)S(1)}, bf16[8,512,512]{2,1,0:T(8,128)(2,1)}, u32[]{:S(2)}) copy-start(bf16[8,512,512]{2,1,0:T(8,128)(2,1)} %copy-done) | copy-start | bytes 12582916
  134.9 2.1 copy-start.5
  208.7 8.5 %copy-start.9 = (f32[8,128,128]{2,1,0:T(8,128)S(1)}, f32[8,128,128]{2,1,0:T(8,128)}, u32[]{:S(2)}) copy-start(f32[8,128,128]{2,1,0:T(8,128)} %fusion.15) | copy-start | bytes 1572868
  217.1 2.3 copy-start.8
  217.2 3.2 %copy-start.6 = (bf16[8,128,512]{2,1,0:T(8,128)(2,1)S(1)}, bf16[8,128,512]{2,1,0:T(8,128)(2,1)}, u32[]{:S(2)}) copy-start(bf16[8,128,512]{2,1,0:T(8,128)(2,1)} %add_convert_fusion.2) | copy-start | bytes 3145732
  219.5 1.0 copy-start.7
  220.9 5.6 %collective-permute-start.1 = (bf16[3,2,1024]{2,1,0:T(2,128)(2,1)S(1)}, bf16[3,2,1024]{2,1,0:T(2,128)(2,1)S(1)}, u32[]{:S(2)}, u32[]{:S(2)}) collective-permute-start(bf16[3,2,1024]{2,1,0:T(2,128)(2,1)S(1)} %copy.61), channel_id=1, source_target_pairs={{4,0},{8,4},{12,8},{16,12},{20,16},{24,20},{28,24},{5,1},{9,5},{13... | collective-permute-start | bytes 36872 | tf_op jit(solution)/shard_map/ppermute | solution.py:14
Sparse Core Ops, SparseCore 0:
  30.1 73.0 all-gather.6
  129.7 78.9 all-gather.8
